TPU v7x, 32 devices: a whole 2x2x4 slice. The times are simulated.
32 devices in a mesh: pairs: 2 (over y), ctx: 8 (over z, x), head: 2 (over core).
Axes of the slice: x: 2, y: 2, z: 4, core: 2. Of those that a mesh axis runs over, the one named last changes fastest.
Arguments:
- hidden: bfloat16 [16, 2, 8192], P(('pairs', 'ctx')), parts along dimension 0, may hold values from -6 to 6
- wq: bfloat16 [8192, 4096], P('ctx', 'head'), may hold values from -0.0625 to 0.0625
- wkv: bfloat16 [2, 8192, 512], P(None, 'ctx', 'head'), may hold values from -0.0625 to 0.0625
- bias_q: bfloat16 [4096], P('head'), may hold values from -5.2 to 5.2
- bias_kv: bfloat16 [2, 512], P(None, 'head'), may hold values from -5.2 to 5.2
- key_value_cache: bfloat16 [2, 8192, 512], P(None, ('pairs', 'ctx'), 'head'), parts along dimension 1, may hold values from -46 to 46, as said below
- prompt_len: int32 [2], P('pairs'), parts along dimension 0, may hold values from 512 to 4096
- resp_len: int32 [4], P('pairs'), parts along dimension 0, may hold values from 2 to 8
Outputs:
- attn_out: bfloat16 [16, 2, 4096], P(('pairs', 'ctx'), None, 'head'), parts along dimension 0
There are 2 independent parts, one for each index of `pairs`. A program takes and returns all parts, laid end to end along the dimension named above; an argument that names none is the same for every part. Nothing has to cross between parts.
Inputs may be any that keep to these rules, and one draw needn't show every extreme that they name: `key_value_cache`: entries beyond prompt_len are padding and must not be attended to. Prompt positions from prompt_len on are padding. Token slots of response r from resp_len[r] on are padding.
All inputs are finite; a program needn't handle non-finite values.
Results may differ from a plain program's by a relative error of at most 0.025.
Values may be sent and summed in bfloat16 or wider, within the bound.
No kernel may reach another device: no remote copies, remote signals or barrier semaphores. Data moves between devices by JAX's collectives and lax.ppermute only.
A program may use at most 64 MiB of HBM per device.

v0:
```python
import jax
import jax.numpy as jnp
from jax import lax
from jax.sharding import PartitionSpec as P

HEAD_SIZE = 128
NEG_FILL = -1e30


def shards(hidden, wq, wkv, bias_q, bias_kv, key_value_cache, prompt_len, resp_len):
    tok_dev = hidden.shape[0]
    ctx_index = lax.axis_index("ctx")
    resp_tokens = tok_dev * lax.axis_size("ctx")
    q_width = wq.shape[1]
    k_width = wkv.shape[2]
    kv_local = k_width // HEAD_SIZE
    query_group_width = q_width // k_width
    score_scale = HEAD_SIZE ** (-0.5)
    row_count = 2 * tok_dev
    columns = lax.all_to_all(hidden, "ctx", split_axis=2, concat_axis=0, tiled=True)
    flat_rows = columns.reshape(2 * resp_tokens, columns.shape[2])
    weights_all = jnp.concatenate((wq, wkv[0], wkv[1]), axis=1)
    bias_all = jnp.concatenate((bias_q, bias_kv[0], bias_kv[1])).astype(jnp.float32)
    summed = lax.psum(jnp.dot(flat_rows, weights_all, preferred_element_type=jnp.float32), "ctx")
    projected = (summed + bias_all).astype(jnp.bfloat16)
    owned = lax.dynamic_slice_in_dim(projected, ctx_index * row_count, row_count, 0)
    query_rows = projected[:, :q_width].reshape(
        2 * resp_tokens, kv_local, query_group_width, HEAD_SIZE
    )
    cache_len = key_value_cache.shape[1]
    key_block = min(512, cache_len)
    block_count = cache_len // key_block
    prompt_key_rows = key_value_cache[0].reshape(block_count, key_block, kv_local, HEAD_SIZE)
    prompt_value_rows = key_value_cache[1].reshape(block_count, key_block, kv_local, HEAD_SIZE)
    first_slot = ctx_index * cache_len
    live_limit = prompt_len[0]

    def visit(carry, inputs):
        running_max, running_sum, weighted = carry
        block_keys, block_values, block_index = inputs
        scores = (
            jnp.einsum("rgjd,kgd->grjk", query_rows, block_keys, preferred_element_type=jnp.float32)
            * score_scale
        )
        position = first_slot + block_index * key_block + lax.iota(jnp.int32, key_block)
        is_live = position < live_limit
        scores = jnp.where(is_live, scores, NEG_FILL)
        new_max = jnp.maximum(running_max, jnp.max(scores, axis=-1))
        unscaled = jnp.where(is_live, jnp.exp(scores - new_max[..., None]), 0.0)
        factor = jnp.exp(running_max - new_max)
        running_sum = running_sum * factor + jnp.sum(unscaled, axis=-1)
        weighted = weighted * factor[..., None] + jnp.einsum(
            "grjk,kgd->grjd",
            unscaled.astype(jnp.bfloat16),
            block_values,
            preferred_element_type=jnp.float32,
        )
        return ((new_max, running_sum, weighted), None)

    statistic_shape = (kv_local, 2 * resp_tokens, query_group_width)
    start_state = (
        jnp.full(statistic_shape, NEG_FILL, jnp.float32),
        jnp.zeros(statistic_shape, jnp.float32),
        jnp.zeros(statistic_shape + (HEAD_SIZE,), jnp.float32),
    )
    closing_state, unused = lax.scan(
        visit,
        start_state,
        (prompt_key_rows, prompt_value_rows, jnp.arange(block_count, dtype=jnp.int32)),
    )
    owned_q = owned[:, :q_width].reshape(tok_dev, 2, kv_local, query_group_width, HEAD_SIZE)
    fresh_key_rows = projected[:, q_width : q_width + k_width].reshape(
        resp_tokens, 2, kv_local, HEAD_SIZE
    )
    fresh_value_rows = projected[:, q_width + k_width :].reshape(
        resp_tokens, 2, kv_local, HEAD_SIZE
    )
    self_scores = (
        jnp.einsum("trgjd,urgd->gtrju", owned_q, fresh_key_rows, preferred_element_type=jnp.float32)
        * score_scale
    )
    token_pos = ctx_index * tok_dev + lax.iota(jnp.int32, tok_dev)
    key_pos = lax.iota(jnp.int32, resp_tokens)
    self_live = (key_pos[None, None, :] <= token_pos[:, None, None]) & (
        key_pos[None, None, :] < resp_len[None, :, None]
    )
    self_live = self_live[None, :, :, None, :]
    self_scores = jnp.where(self_live, self_scores, NEG_FILL)
    self_max = jnp.max(self_scores, axis=-1)
    self_weights = jnp.where(self_live, jnp.exp(self_scores - self_max[..., None]), 0.0)
    self_sum = jnp.sum(self_weights, axis=-1)
    self_acc = jnp.einsum(
        "gtrju,urgd->gtrjd",
        self_weights.astype(jnp.bfloat16),
        fresh_value_rows,
        preferred_element_type=jnp.float32,
    )
    lead_shape = (1, kv_local, resp_tokens, 2, query_group_width)
    remote_max, remote_sum, remote_acc = (
        lax.all_to_all(
            closing_state[0].reshape(lead_shape), "ctx", split_axis=2, concat_axis=0, tiled=True
        ),
        lax.all_to_all(
            closing_state[1].reshape(lead_shape), "ctx", split_axis=2, concat_axis=0, tiled=True
        ),
        lax.all_to_all(
            closing_state[2].reshape(lead_shape + (HEAD_SIZE,)),
            "ctx",
            split_axis=2,
            concat_axis=0,
            tiled=True,
        ),
    )
    overall = jnp.maximum(jnp.max(remote_max, axis=0), self_max)
    remote_factor = jnp.exp(remote_max - overall[None])
    prompt_acc = jnp.sum(remote_factor[..., None] * remote_acc, axis=0)
    prompt_total = jnp.sum(remote_factor * remote_sum, axis=0)
    self_factor = jnp.exp(self_max - overall)
    numerator = prompt_acc + self_factor[..., None] * self_acc
    denominator = prompt_total + self_factor * self_sum
    result = numerator / denominator[..., None]
    row_live = token_pos[:, None] < resp_len[None, :]
    result = jnp.where(row_live[None, :, :, None, None], result, 0.0)
    return jnp.transpose(result, (1, 2, 0, 3, 4)).reshape(tok_dev, 2, q_width).astype(jnp.bfloat16)


def solution(mesh):
    return jax.shard_map(
        shards,
        mesh=mesh,
        in_specs=(
            P(("pairs", "ctx"), None, None),
            P("ctx", "head"),
            P(None, "ctx", "head"),
            P("head"),
            P(None, "head"),
            P(None, ("pairs", "ctx"), "head"),
            P("pairs"),
            P("pairs"),
        ),
        out_specs=P(("pairs", "ctx"), None, "head"),
        check_vma=False,
    )
```

profile of v0, /device:TPU:0, one launch (start us, length us, event | category | flops | bytes accessed | tf_op | source)
XLA Modules:
  0.0 205.0 jit_solution(12979786244044143791)
XLA Ops:
  6.5 8.2 %copy.38 = bf16[1,2,8192]{1,0,2:T(2,128)(2,1)} copy(bf16[1,2,8192]{2,1,0:T(2,128)(2,1)} %param.8) | data formatting | bytes 65536 | tf_op args[0]
  14.8 0.5 broadcast.132
  15.3 0.0 copy-start
  15.3 45.3 %reduce.10 = bf16[8192,2]{1,0:T(8,128)(2,1)S(1)} reduce(bf16[8192,1,2]{2,1,0:T(2,128)(2,1)} %bitcast.123, bf16[]{:T(256)} %broadcast.132), dimensions={1}, to_apply=%bitcast.111.reduce_sub_computation | reduce | bytes 65538
  60.6 0.0 copy-start.3
  60.6 0.0 copy-start.2
  60.6 3.8 %reshape.289 = bf16[8,2,1024]{2,1,0:T(2,128)(2,1)} reshape(bf16[8192,2]{1,0:T(8,128)(2,1)S(1)} %reduce.10) | data formatting | bytes 65536
  64.4 7.3 %all-to-all-start = ((bf16[8,2,1024]{2,1,0:T(2,128)(2,1)}), bf16[8,2,1024]{2,1,0:T(2,128)(2,1)S(1)}, u32[]{:S(2)}, u32[]{:S(2)}) async-start(bf16[8,2,1024]{2,1,0:T(2,128)(2,1)} %reshape.289), calls=%async_computation | async-start | bytes 65536 | tf_op jit(solution)/shard_map/all_to_all | solution.py:20
  71.7 0.0 all-reduce.2.cloned.1.call-start
  71.8 1.1 fusion.45
  72.8 0.0 copy-done
  72.8 0.1 slice_bitcast_fusion.1
  73.6 0.0 copy-done.3
  73.6 0.1 compare_and_fusion
  73.7 0.0 copy-done.2
  73.7 4.7 %all-to-all-done = bf16[8,2,1024]{2,1,0:T(2,128)(2,1)S(1)} async-done(((bf16[8,2,1024]{2,1,0:T(2,128)(2,1)}), bf16[8,2,1024]{2,1,0:T(2,128)(2,1)S(1)}, u32[]{:S(2)}, u32[]{:S(2)}) %all-to-all-start) | async-done | bytes 32800 | tf_op jit(solution)/shard_map/all_to_all | solution.py:20
  78.4 6.3 %reshape.290 = bf16[8192,1,2]{2,1,0:T(2,128)(2,1)} reshape(bf16[8,2,1024]{2,1,0:T(2,128)(2,1)S(1)} %all-to-all-done) | data formatting | bytes 65536
  84.7 8.1 %copy.39 = bf16[1,2,8192]{2,1,0:T(2,128)(2,1)S(1)} copy(bf16[1,2,8192]{1,0,2:T(2,128)(2,1)} %bitcast.124) | data formatting | bytes 65536 | tf_op jit(solution)/shard_map/all_to_all | solution.py:20
  92.8 0.0 copy-start.1
  92.9 3.3 %fusion.6 = f32[16,2560]{1,0:T(8,128)} fusion(bf16[16,1024]{1,0:T(8,128)(2,1)S(1)} %reshape.278, bf16[1024,256]{1,0:T(8,128)(2,1)S(1)} %get-tuple-element.26, bf16[1024,256]{1,0:T(8,128)(2,1)S(1)} %get-tuple-element.25, bf16[1024,2048]{1,0:T(8,128)(2,1)} %param.9), kind=kOutput, calls=%fused_computation.6 | convolution fusion | flops 99614720 | bytes 5439488 | tf_op jit(solution)/shard_map/dot_general | solution.py:24
  96.2 0.0 all-reduce.2.cloned.1.call-update
  96.2 0.1 copy.62
  96.4 0.1 copy.61
  96.5 0.0 copy-done.1
  96.6 67.2 %all-reduce.2.cloned.1.call-done = f32[16,2560]{1,0:T(8,128)} async-done(((f32[16,2560]{1,0:T(8,128)}), f32[16,2560]{1,0:T(8,128)}) %all-reduce.2.cloned.1.call-update) | async-done | bytes 163856 | tf_op jit(solution)/shard_map/psum | solution.py:24
  163.8 0.9 add_convert_fusion
  164.7 0.3 fusion.47
  165.1 0.6 copy.44
  165.7 4.4 %all-to-all-start.1 = ((f32[1,2,8,2,8]{4,3,1,0,2:T(2,128)}), f32[1,2,8,2,8]{4,3,1,0,2:T(2,128)S(1)}, u32[]{:S(2)}, u32[]{:S(2)}) async-start(f32[1,2,8,2,8]{4,3,1,0,2:T(2,128)} %copy.44), calls=%async_computation.1 | async-start | bytes 32768 | tf_op jit(solution)/shard_map/all_to_all | solution.py:100
  170.1 0.2 fusion.18
  170.4 0.3 convolution_add_fusion
  170.6 0.1 fusion.48
  170.8 0.1 fusion.29
  170.9 0.6 copy.49
  171.5 0.6 copy.52
  172.1 4.5 %all-to-all-done.1 = f32[1,2,8,2,8]{4,3,1,0,2:T(2,128)S(1)} async-done(((f32[1,2,8,2,8]{4,3,1,0,2:T(2,128)}), f32[1,2,8,2,8]{4,3,1,0,2:T(2,128)S(1)}, u32[]{:S(2)}, u32[]{:S(2)}) %all-to-all-start.1) | async-done | bytes 1056 | tf_op jit(solution)/shard_map/all_to_all | solution.py:100
  176.6 3.3 %all-to-all-start.3 = ((f32[1,2,8,2,8]{4,3,1,0,2:T(2,128)}), f32[1,2,8,2,8]{4,3,1,0,2:T(2,128)S(1)}, u32[]{:S(2)}, u32[]{:S(2)}) async-start(f32[1,2,8,2,8]{4,3,1,0,2:T(2,128)} %copy.52), calls=%async_computation.3 | async-start | bytes 32768 | tf_op jit(solution)/shard_map/all_to_all | solution.py:103
  180.0 6.5 %all-to-all-done.3 = f32[1,2,8,2,8]{4,3,1,0,2:T(2,128)S(1)} async-done(((f32[1,2,8,2,8]{4,3,1,0,2:T(2,128)}), f32[1,2,8,2,8]{4,3,1,0,2:T(2,128)S(1)}, u32[]{:S(2)}, u32[]{:S(2)}) %all-to-all-start.3) | async-done | bytes 1056 | tf_op jit(solution)/shard_map/all_to_all | solution.py:103
  186.5 3.4 %all-to-all-start.2 = ((f32[1,2,8,2,8,128]{5,4,3,1,0,2:T(8,128)}), f32[1,2,8,2,8,128]{5,4,3,1,0,2:T(8,128)S(1)}, u32[]{:S(2)}, u32[]{:S(2)}) async-start(f32[1,2,8,2,8,128]{5,4,3,1,0,2:T(8,128)} %copy.49), calls=%async_computation.2 | async-start | bytes 262144 | tf_op jit(solution)/shard_map/all_to_all | solution.py:106
  190.0 7.2 %all-to-all-done.2 = f32[1,2,8,2,8,128]{5,4,3,1,0,2:T(8,128)S(1)} async-done(((f32[1,2,8,2,8,128]{5,4,3,1,0,2:T(8,128)}), f32[1,2,8,2,8,128]{5,4,3,1,0,2:T(8,128)S(1)}, u32[]{:S(2)}, u32[]{:S(2)}) %all-to-all-start.2) | async-done | bytes 131104 | tf_op jit(solution)/shard_map/all_to_all | solution.py:106
  197.2 0.1 fusion.24
  197.3 0.2 fusion.15
  197.5 0.6 convert_element_type.36
  (22 shorter events, 0.3 us)
Async XLA Ops:
  15.3 57.6 %copy-start = (bf16[2,1024,256]{2,1,0:T(8,128)(2,1)S(1)}, bf16[2,1024,256]{2,1,0:T(8,128)(2,1)}, u32[]{:S(2)}) copy-start(bf16[2,1024,256]{2,1,0:T(8,128)(2,1)} %param.10) | copy-start | bytes 3145732
  60.6 13.0 %copy-start.3 = (s32[2]{0:T(128)S(1)}, s32[2]{0:T(128)}, u32[]{:S(2)}) copy-start(s32[2]{0:T(128)} %param.15) | copy-start | bytes 28
  60.6 13.1 %copy-start.2 = (bf16[2,256]{1,0:T(2,128)(2,1)S(1)}, bf16[2,256]{1,0:T(2,128)(2,1)}, u32[]{:S(2)}) copy-start(bf16[2,256]{1,0:T(2,128)(2,1)} %param.12) | copy-start | bytes 3076
  64.4 14.0 %all-to-all-start = ((bf16[8,2,1024]{2,1,0:T(2,128)(2,1)}), bf16[8,2,1024]{2,1,0:T(2,128)(2,1)S(1)}, u32[]{:S(2)}, u32[]{:S(2)}) async-start(bf16[8,2,1024]{2,1,0:T(2,128)(2,1)} %reshape.289), calls=%async_computation | async-start | bytes 65536 | tf_op jit(solution)/shard_map/all_to_all | solution.py:20
  71.7 92.0 %all-reduce.2.cloned.1.call-start = ((), (), s32[]{:S(2)}) async-start(), calls=%async_computation.4 | async-start | bytes 327680 | tf_op jit(solution)/shard_map/psum | solution.py:24
  92.8 3.7 %copy-start.1 = (bf16[2048]{0:T(1024)(128)(2,1)S(1)}, bf16[2048]{0:T(1024)(128)(2,1)}, u32[]{:S(2)}) copy-start(bf16[2048]{0:T(1024)(128)(2,1)} %param.11) | copy-start | bytes 12292
  165.7 11.0 %all-to-all-start.1 = ((f32[1,2,8,2,8]{4,3,1,0,2:T(2,128)}), f32[1,2,8,2,8]{4,3,1,0,2:T(2,128)S(1)}, u32[]{:S(2)}, u32[]{:S(2)}) async-start(f32[1,2,8,2,8]{4,3,1,0,2:T(2,128)} %copy.44), calls=%async_computation.1 | async-start | bytes 32768 | tf_op jit(solution)/shard_map/all_to_all | solution.py:100
  176.6 9.9 %all-to-all-start.3 = ((f32[1,2,8,2,8]{4,3,1,0,2:T(2,128)}), f32[1,2,8,2,8]{4,3,1,0,2:T(2,128)S(1)}, u32[]{:S(2)}, u32[]{:S(2)}) async-start(f32[1,2,8,2,8]{4,3,1,0,2:T(2,128)} %copy.52), calls=%async_computation.3 | async-start | bytes 32768 | tf_op jit(solution)/shard_map/all_to_all | solution.py:103
  186.5 10.7 %all-to-all-start.2 = ((f32[1,2,8,2,8,128]{5,4,3,1,0,2:T(8,128)}), f32[1,2,8,2,8,128]{5,4,3,1,0,2:T(8,128)S(1)}, u32[]{:S(2)}, u32[]{:S(2)}) async-start(f32[1,2,8,2,8,128]{5,4,3,1,0,2:T(8,128)} %copy.49), calls=%async_computation.2 | async-start | bytes 262144 | tf_op jit(solution)/shard_map/all_to_all | solution.py:106
Sparse Core Ops, SparseCore 0:
  96.3 67.3 all-reduce.1
where the time goes:
time: 206 us; the launch traced here: 205 us
  waiting for transfers between devices  90.1 us (44%)
  other arithmetic  46.9 us (23%)
  local copies, waits for them, and re-layouts  31 us (15%)
  starting transfers between devices  18.4 us (9%)
  between operations  14.3 us (7%)
  matrix products  4.29 us (2%)
    psum x1, waiting for transfers between devices, shards(): lax.psum(jnp.dot(flat_rows, weights_all, preferred_element_type=jnp.float...  67.2 us
    unnamed x1, other arithmetic  45.3 us
    unnamed x18, local copies, waits for them, and re-layouts  19.2 us
    all_to_all x2, local copies, waits for them, and re-layouts, shards(): lax.all_to_all(hidden, 'ctx', split_axis=2, concat_axis=0, tiled=True)  8.11 us
    all_to_all x1, starting transfers between devices, shards(): lax.all_to_all(hidden, 'ctx', split_axis=2, concat_axis=0, tiled=True)  7.28 us
    all_to_all x1, waiting for transfers between devices, shards(): lax.all_to_all(closing_state[2].reshape(lead_shape + (HEAD_SIZE,)), 'ctx'...  7.2 us
    all_to_all x1, waiting for transfers between devices, shards(): lax.all_to_all(closing_state[1].reshape(lead_shape), 'ctx', split_axis=2,...  6.48 us
    all_to_all x1, waiting for transfers between devices, shards(): lax.all_to_all(hidden, 'ctx', split_axis=2, concat_axis=0, tiled=True)  4.69 us
  transfers between devices with their start and end apart: 5, of which 5 were waited for; matrix products, arithmetic and copies ran while one was open for 2% of the time, Pallas kernels for 0%

commit v1 on v0

--- a/solution.py
+++ b/solution.py
@@ -21,7 +21,10 @@
     flat_rows = columns.reshape(2 * resp_tokens, columns.shape[2])
     weights_all = jnp.concatenate((wq, wkv[0], wkv[1]), axis=1)
     bias_all = jnp.concatenate((bias_q, bias_kv[0], bias_kv[1])).astype(jnp.float32)
-    summed = lax.psum(jnp.dot(flat_rows, weights_all, preferred_element_type=jnp.float32), "ctx")
+    summed = jnp.sum(
+        lax.all_gather(jnp.dot(flat_rows, weights_all, preferred_element_type=jnp.float32), "ctx"),
+        axis=0,
+    )
     projected = (summed + bias_all).astype(jnp.bfloat16)
     owned = lax.dynamic_slice_in_dim(projected, ctx_index * row_count, row_count, 0)
     query_rows = projected[:, :q_width].reshape(

time: 206 us -> 177 us (0.86)
  waiting for transfers between devices: 90.1 us -> 62.9 us
    psum x1 -> x0, waiting for transfers between devices: 67.2 us -> none  [shards(): lax.psum(jnp.dot(flat_rows, weights_all, preferred_element_type=jnp.float...]
    all_gather x0 -> x1, waiting for transfers between devices: none -> 38.2 us  [shards(): lax.all_gather(jnp.dot(flat_rows, weights_all, preferred_element_type=jnp...]
    unnamed x18 -> x20, local copies, waits for them, and re-layouts: 19.2 us -> 19.2 us
where the time goes in v1:
time: 177 us; the launch traced here: 176 us
  waiting for transfers between devices  62.9 us (36%)
  other arithmetic  47.4 us (27%)
  local copies, waits for them, and re-layouts  30 us (17%)
  starting transfers between devices  17.5 us (10%)
  between operations  14.3 us (8%)
  matrix products  4.35 us (2%)
    unnamed x1, other arithmetic  45.3 us
    all_gather x1, waiting for transfers between devices, shards(): lax.all_gather(jnp.dot(flat_rows, weights_all, preferred_element_type=jnp...  38.2 us
    unnamed x20, local copies, waits for them, and re-layouts  19.2 us
    all_to_all x2, local copies, waits for them, and re-layouts, shards(): lax.all_to_all(hidden, 'ctx', split_axis=2, concat_axis=0, tiled=True)  8.11 us
    all_to_all x1, starting transfers between devices, shards(): lax.all_to_all(hidden, 'ctx', split_axis=2, concat_axis=0, tiled=True)  7.28 us
    all_to_all x1, waiting for transfers between devices, shards(): lax.all_to_all(closing_state[2].reshape(lead_shape + (HEAD_SIZE,)), 'ctx'...  7.2 us
    all_to_all x1, waiting for transfers between devices, shards(): lax.all_to_all(hidden, 'ctx', split_axis=2, concat_axis=0, tiled=True)  6.55 us
    all_to_all x1, waiting for transfers between devices, shards(): lax.all_to_all(closing_state[1].reshape(lead_shape), 'ctx', split_axis=2,...  6.48 us
  transfers between devices with their start and end apart: 5, of which 5 were waited for; matrix products, arithmetic and copies ran while one was open for 2% of the time, Pallas kernels for 0%

profile of v1, /device:TPU:0, one launch (start us, length us, event | category | flops | bytes accessed | tf_op | source)
XLA Modules:
  0.0 176.4 jit_solution(12124132653678122860)
XLA Ops:
  6.5 8.2 %copy.34 = bf16[1,2,8192]{1,0,2:T(2,128)(2,1)} copy(bf16[1,2,8192]{2,1,0:T(2,128)(2,1)} %param.8) | data formatting | bytes 65536 | tf_op args[0]
  14.8 0.5 broadcast.132
  15.3 0.0 copy-start
  15.3 45.3 %reduce.10 = bf16[8192,2]{1,0:T(8,128)(2,1)S(1)} reduce(bf16[8192,1,2]{2,1,0:T(2,128)(2,1)} %bitcast.124, bf16[]{:T(256)} %broadcast.132), dimensions={1}, to_apply=%bitcast.112.reduce_sub_computation | reduce | bytes 65538
  60.6 3.8 %reshape.290 = bf16[8,2,1024]{2,1,0:T(2,128)(2,1)} reshape(bf16[8192,2]{1,0:T(8,128)(2,1)S(1)} %reduce.10) | data formatting | bytes 65536
  64.4 7.3 %all-to-all-start = ((bf16[8,2,1024]{2,1,0:T(2,128)(2,1)}), bf16[8,2,1024]{2,1,0:T(2,128)(2,1)S(1)}, u32[]{:S(2)}, u32[]{:S(2)}) async-start(bf16[8,2,1024]{2,1,0:T(2,128)(2,1)} %reshape.290), calls=%async_computation | async-start | bytes 65536 | tf_op jit(solution)/shard_map/all_to_all | solution.py:20
  71.7 0.0 all-gather.3.cloned.1.call-start
  71.7 0.0 copy-done
  71.8 0.1 slice_bitcast_fusion.1
  71.8 6.6 %all-to-all-done = bf16[8,2,1024]{2,1,0:T(2,128)(2,1)S(1)} async-done(((bf16[8,2,1024]{2,1,0:T(2,128)(2,1)}), bf16[8,2,1024]{2,1,0:T(2,128)(2,1)S(1)}, u32[]{:S(2)}, u32[]{:S(2)}) %all-to-all-start) | async-done | bytes 32800 | tf_op jit(solution)/shard_map/all_to_all | solution.py:20
  78.4 6.3 %reshape.291 = bf16[8192,1,2]{2,1,0:T(2,128)(2,1)} reshape(bf16[8,2,1024]{2,1,0:T(2,128)(2,1)S(1)} %all-to-all-done) | data formatting | bytes 65536
  84.7 8.1 %copy.35 = bf16[1,2,8192]{2,1,0:T(2,128)(2,1)S(1)} copy(bf16[1,2,8192]{1,0,2:T(2,128)(2,1)} %bitcast.125) | data formatting | bytes 65536 | tf_op jit(solution)/shard_map/all_to_all | solution.py:20
  92.8 0.0 copy-start.1
  92.8 0.0 copy-start.3
  92.8 0.0 copy-start.2
  92.9 0.0 copy-start.4
  92.9 3.4 %fusion.6 = f32[16,2560]{1,0:T(8,128)} fusion(bf16[16,1024]{1,0:T(8,128)(2,1)S(1)} %reshape.278, bf16[1024,256]{1,0:T(8,128)(2,1)S(1)} %get-tuple-element.26, bf16[1024,256]{1,0:T(8,128)(2,1)S(1)} %get-tuple-element.25, bf16[1024,2048]{1,0:T(8,128)(2,1)} %param.9), kind=kOutput, calls=%fused_computation.6 | convolution fusion | flops 99614720 | bytes 5439488 | tf_op jit(solution)/shard_map/dot_general | solution.py:25
  96.3 0.0 all-gather.3.cloned.1.call-update
  96.3 0.0 copy-done.1
  96.4 0.1 copy.58
  96.5 0.1 copy.57
  97.3 0.0 copy-done.3
  97.4 0.0 copy-done.2
  97.4 0.0 copy-done.4
  97.4 0.1 compare_and_fusion
  97.5 38.2 %all-gather.3.cloned.1.call-done = f32[128,2560]{1,0:T(8,128)} async-done(((f32[16,2560]{1,0:T(8,128)}), f32[128,2560]{1,0:T(8,128)}) %all-gather.3.cloned.1.call-update) | async-done | bytes 1310736 | tf_op jit(solution)/shard_map/all_gather | solution.py:25
  135.7 1.4 reduce_sum.56
  137.1 0.3 fusion.47
  137.5 0.6 copy.40
  138.1 3.4 %all-to-all-start.1 = ((f32[1,2,8,2,8]{4,3,1,0,2:T(2,128)}), f32[1,2,8,2,8]{4,3,1,0,2:T(2,128)S(1)}, u32[]{:S(2)}, u32[]{:S(2)}) async-start(f32[1,2,8,2,8]{4,3,1,0,2:T(2,128)} %copy.40), calls=%async_computation.1 | async-start | bytes 32768 | tf_op jit(solution)/shard_map/all_to_all | solution.py:103
  141.5 0.2 fusion.18
  141.8 0.3 convolution_add_fusion
  142.1 0.1 fusion.48
  142.2 0.1 fusion.29
  142.3 0.7 copy.45
  143.0 0.6 copy.48
  143.6 4.5 %all-to-all-done.1 = f32[1,2,8,2,8]{4,3,1,0,2:T(2,128)S(1)} async-done(((f32[1,2,8,2,8]{4,3,1,0,2:T(2,128)}), f32[1,2,8,2,8]{4,3,1,0,2:T(2,128)S(1)}, u32[]{:S(2)}, u32[]{:S(2)}) %all-to-all-start.1) | async-done | bytes 1056 | tf_op jit(solution)/shard_map/all_to_all | solution.py:103
  148.1 3.3 %all-to-all-start.3 = ((f32[1,2,8,2,8]{4,3,1,0,2:T(2,128)}), f32[1,2,8,2,8]{4,3,1,0,2:T(2,128)S(1)}, u32[]{:S(2)}, u32[]{:S(2)}) async-start(f32[1,2,8,2,8]{4,3,1,0,2:T(2,128)} %copy.48), calls=%async_computation.3 | async-start | bytes 32768 | tf_op jit(solution)/shard_map/all_to_all | solution.py:106
  151.5 6.5 %all-to-all-done.3 = f32[1,2,8,2,8]{4,3,1,0,2:T(2,128)S(1)} async-done(((f32[1,2,8,2,8]{4,3,1,0,2:T(2,128)}), f32[1,2,8,2,8]{4,3,1,0,2:T(2,128)S(1)}, u32[]{:S(2)}, u32[]{:S(2)}) %all-to-all-start.3) | async-done | bytes 1056 | tf_op jit(solution)/shard_map/all_to_all | solution.py:106
  157.9 3.4 %all-to-all-start.2 = ((f32[1,2,8,2,8,128]{5,4,3,1,0,2:T(8,128)}), f32[1,2,8,2,8,128]{5,4,3,1,0,2:T(8,128)S(1)}, u32[]{:S(2)}, u32[]{:S(2)}) async-start(f32[1,2,8,2,8,128]{5,4,3,1,0,2:T(8,128)} %copy.45), calls=%async_computation.2 | async-start | bytes 262144 | tf_op jit(solution)/shard_map/all_to_all | solution.py:109
  161.4 7.2 %all-to-all-done.2 = f32[1,2,8,2,8,128]{5,4,3,1,0,2:T(8,128)S(1)} async-done(((f32[1,2,8,2,8,128]{5,4,3,1,0,2:T(8,128)}), f32[1,2,8,2,8,128]{5,4,3,1,0,2:T(8,128)S(1)}, u32[]{:S(2)}, u32[]{:S(2)}) %all-to-all-start.2) | async-done | bytes 131104 | tf_op jit(solution)/shard_map/all_to_all | solution.py:109
  168.6 0.1 fusion.24
  168.7 0.2 fusion.15
  168.9 0.6 convert_element_type.36
  (24 shorter events, 0.4 us)
Async XLA Ops:
  15.3 56.5 %copy-start = (bf16[2,1024,256]{2,1,0:T(8,128)(2,1)S(1)}, bf16[2,1024,256]{2,1,0:T(8,128)(2,1)}, u32[]{:S(2)}) copy-start(bf16[2,1024,256]{2,1,0:T(8,128)(2,1)} %param.10) | copy-start | bytes 3145732
  64.4 14.0 %all-to-all-start = ((bf16[8,2,1024]{2,1,0:T(2,128)(2,1)}), bf16[8,2,1024]{2,1,0:T(2,128)(2,1)S(1)}, u32[]{:S(2)}, u32[]{:S(2)}) async-start(bf16[8,2,1024]{2,1,0:T(2,128)(2,1)} %reshape.290), calls=%async_computation | async-start | bytes 65536 | tf_op jit(solution)/shard_map/all_to_all | solution.py:20
  71.7 64.0 %all-gather.3.cloned.1.call-start = ((), (), s32[]{:S(2)}) async-start(), calls=%async_computation.4 | async-start | bytes 1474560 | tf_op jit(solution)/shard_map/all_gather | solution.py:25
  92.8 3.5 %copy-start.1 = (bf16[2,512,256]{2,1,0:T(8,128)(2,1)S(1)}, bf16[2,512,256]{2,1,0:T(8,128)(2,1)}, u32[]{:S(2)}) copy-start(bf16[2,512,256]{2,1,0:T(8,128)(2,1)} %param.13) | copy-start | bytes 1572868
  92.8 4.5 %copy-start.3 = (bf16[2,256]{1,0:T(2,128)(2,1)S(1)}, bf16[2,256]{1,0:T(2,128)(2,1)}, u32[]{:S(2)}) copy-start(bf16[2,256]{1,0:T(2,128)(2,1)} %param.12) | copy-start | bytes 3076
  92.8 4.5 %copy-start.2 = (bf16[2048]{0:T(1024)(128)(2,1)S(1)}, bf16[2048]{0:T(1024)(128)(2,1)}, u32[]{:S(2)}) copy-start(bf16[2048]{0:T(1024)(128)(2,1)} %param.11) | copy-start | bytes 12292
  92.9 4.5 %copy-start.4 = (s32[2]{0:T(128)S(1)}, s32[2]{0:T(128)}, u32[]{:S(2)}) copy-start(s32[2]{0:T(128)} %param.15) | copy-start | bytes 28
  138.1 10.0 %all-to-all-start.1 = ((f32[1,2,8,2,8]{4,3,1,0,2:T(2,128)}), f32[1,2,8,2,8]{4,3,1,0,2:T(2,128)S(1)}, u32[]{:S(2)}, u32[]{:S(2)}) async-start(f32[1,2,8,2,8]{4,3,1,0,2:T(2,128)} %copy.40), calls=%async_computation.1 | async-start | bytes 32768 | tf_op jit(solution)/shard_map/all_to_all | solution.py:103
  148.1 9.9 %all-to-all-start.3 = ((f32[1,2,8,2,8]{4,3,1,0,2:T(2,128)}), f32[1,2,8,2,8]{4,3,1,0,2:T(2,128)S(1)}, u32[]{:S(2)}, u32[]{:S(2)}) async-start(f32[1,2,8,2,8]{4,3,1,0,2:T(2,128)} %copy.48), calls=%async_computation.3 | async-start | bytes 32768 | tf_op jit(solution)/shard_map/all_to_all | solution.py:106
  157.9 10.7 %all-to-all-start.2 = ((f32[1,2,8,2,8,128]{5,4,3,1,0,2:T(8,128)}), f32[1,2,8,2,8,128]{5,4,3,1,0,2:T(8,128)S(1)}, u32[]{:S(2)}, u32[]{:S(2)}) async-start(f32[1,2,8,2,8,128]{5,4,3,1,0,2:T(8,128)} %copy.45), calls=%async_computation.2 | async-start | bytes 262144 | tf_op jit(solution)/shard_map/all_to_all | solution.py:109
Sparse Core Ops, SparseCore 0:
  96.4 39.2 all-gather.2
